TPU v7x, 32 devices: a whole 2x2x4 slice. The times are simulated.
32 devices in a mesh: tm: 8 (over z, x), gx: 4 (over y, core).
Axes of the slice: x: 2, y: 2, z: 4, core: 2. Of those that a mesh axis runs over, the one named last changes fastest.
Arguments:
- initial: float32 [8, 256, 256], P('gx'), may hold values from -1 to 1
- node_values: float32 [8, 3, 8, 256, 256], P('tm', None, 'gx'), may hold values from -1 to 1
Outputs:
- solution: float32 [8, 3, 8, 256, 256], P('tm', None, 'gx')
All inputs are finite; a program needn't handle non-finite values.
Results may differ from a plain program's by a relative error of at most 0.0002.
Values sent between devices are 32-bit elements; how exact they have to be, the bound alone decides.
No kernel may reach another device: no remote copies, remote signals or barrier semaphores. Data moves between devices by JAX's collectives and lax.ppermute only.
A program may use at most 64 MiB of HBM per device.

v0:
```python
import math

import jax
import jax.numpy as jnp
from jax import lax
from jax.sharding import PartitionSpec as P

SWEEPS = 2


spacing = 2.0
step_size = 0.2
half_step = 0.1


def padded_2(cells, sides, width):
    for axis, dim in sides:
        count = lax.axis_size(axis)
        head = lax.slice_in_dim(cells, 0, width, axis=dim)
        tail = lax.slice_in_dim(cells, cells.shape[dim] - width, cells.shape[dim], axis=dim)
        cells = jnp.concatenate(
            [
                lax.ppermute(tail, axis, [(i, (i + 1) % count) for i in range(count)]),
                cells,
                lax.ppermute(head, axis, [((i + 1) % count, i) for i in range(count)]),
            ],
            axis=dim,
        )
    return cells


def passed_along(shard, axis, by):
    length = lax.axis_size(axis)
    pairs = [(i, i + by) for i in range(length) if 0 <= i + by < length]
    return lax.ppermute(shard, axis, pairs)


def second_derivative(count):
    positions = jnp.arange(count, dtype=jnp.int32)
    offset = positions[None, :] - positions[:, None]
    angle_step = 2.0 * math.pi / count
    parity = jnp.where(offset % 2 == 0, 1.0, -1.0).astype(jnp.float32)
    safe = jnp.where(offset == 0, 1, offset).astype(jnp.float32)
    sine_value = jnp.sin(safe * (angle_step / 2.0))
    off_value = -0.5 * parity / (sine_value * sine_value)
    diagonal_value = -math.pi**2 / (3.0 * angle_step * angle_step) - 1.0 / 6.0
    matrix = jnp.where(offset == 0, jnp.float32(diagonal_value), off_value)
    return matrix * (angle_step / spacing) ** 2


def evaluate(state_field, matrix_y, matrix_z):
    padded = padded_2(state_field, (("gx", 0),), 2)
    term_y = jnp.einsum("jk,xkz->xjz", matrix_y, state_field, precision=lax.Precision.HIGHEST)
    term_z = jnp.einsum("xyk,kz->xyz", state_field, matrix_z, precision=lax.Precision.HIGHEST)
    across = (
        -(padded[:-4] + padded[4:]) + 16.0 * (padded[1:-3] + padded[3:-1]) - 30.0 * state_field
    ) / 12.0
    return across + term_y + term_z + state_field - state_field * state_field * state_field


def local(initial, node_values):
    matrix_y = second_derivative(node_values.shape[3])
    matrix_z = second_derivative(node_values.shape[4])
    leading = lax.axis_index("tm") == 0
    values = [node_values[0, 0], node_values[0, 1], node_values[0, 2]]
    forces = [evaluate(item, matrix_y, matrix_z) for item in values]
    for sweep_index in range(SWEEPS):
        quadrature_one = step_size * (
            5.0 / 24.0 * forces[0] + 1.0 / 3.0 * forces[1] - 1.0 / 24.0 * forces[2]
        )
        quadrature_two = step_size * (
            -1.0 / 24.0 * forces[0] + 1.0 / 3.0 * forces[1] + 5.0 / 24.0 * forces[2]
        )
        arrived = passed_along(values[2], "tm", 1)
        first_node = jnp.where(leading, initial, arrived)
        first_force = evaluate(first_node, matrix_y, matrix_z)
        middle = first_node + half_step * (first_force - forces[0]) + quadrature_one
        middle_force = evaluate(middle, matrix_y, matrix_z)
        final_node = middle + half_step * (middle_force - forces[1]) + quadrature_two
        values = [first_node, middle, final_node]
        if sweep_index + 1 < SWEEPS:
            forces = [first_force, middle_force, evaluate(final_node, matrix_y, matrix_z)]
    return jnp.stack(values, axis=0)[None]


def solution(mesh):
    in_specs = (P("gx", None, None), P("tm", None, "gx", None, None))
    out_specs = P("tm", None, "gx", None, None)
    return jax.shard_map(local, mesh=mesh, in_specs=in_specs, out_specs=out_specs, check_vma=False)
```

profile of v0, /device:TPU:29, one launch (start us, length us, event | category | flops | bytes accessed | tf_op | source)
XLA Modules:
  0.0 122.3 jit_solution(16129979611841570547)
XLA Ops:
  4.3 1.7 %collective-permute-start.3 = (f32[2,256,256]{1,2,0:T(8,128)}, f32[2,256,256]{1,2,0:T(8,128)}, u32[]{:S(2)}, u32[]{:S(2)}) collective-permute-start(f32[2,256,256]{1,2,0:T(8,128)} %bitcast.3), channel_id=1, source_target_pairs={{0,1},{1,2},{2,3},{3,0},{4,5},{5,6},{6,7},{7,4},{8,9},{9,10},{10,1... | collective-permute-start | bytes 1572872 | tf_op jit(solution)/shard_map/ppermute | solution.py:23
  6.2 3.1 %collective-permute-start = (f32[2,256,256]{1,2,0:T(8,128)S(1)}, f32[2,256,256]{1,2,0:T(8,128)}, u32[]{:S(2)}, u32[]{:S(2)}) collective-permute-start(f32[2,256,256]{1,2,0:T(8,128)S(1)} %bitcast.128), channel_id=1, source_target_pairs={{0,4},{4,8},{8,12},{12,16},{16,20},{20,24},{24,28},{1,5},{5,9},{9,... | collective-permute-start | bytes 1572872 | tf_op jit(solution)/shard_map/ppermute | solution.py:35
  9.3 2.7 %convolution_bitcast_fusion.7 = f32[2,256,256]{1,2,0:T(8,128)} fusion(f32[1,3,2,256,256]{4,3,2,1,0:T(8,128)S(1)} %copy-done), kind=kOutput, calls=%fused_computation.8 | convolution fusion | flops 404160512 | bytes 1048576 | tf_op jit(solution)/shard_map/jk,xkz->xjz/dot_general | solution.py:53
  12.0 2.7 %convolution_bitcast_fusion.9 = f32[2,256,256]{1,2,0:T(8,128)} fusion(f32[1,3,2,256,256]{4,3,2,1,0:T(8,128)S(1)} %copy-done), kind=kOutput, calls=%fused_computation.10 | convolution fusion | flops 404160512 | bytes 1048576 | tf_op jit(solution)/shard_map/jk,xkz->xjz/dot_general | solution.py:53
  14.9 1.9 %convolution_bitcast_fusion.5 = f32[2,256,256]{1,2,0:T(8,128)S(1)} fusion(f32[1,3,2,256,256]{4,3,2,1,0:T(8,128)S(1)} %copy-done), kind=kOutput, calls=%fused_computation.6 | convolution fusion | flops 404160512 | bytes 1048576 | tf_op jit(solution)/shard_map/jk,xkz->xjz/dot_general | solution.py:53
  16.8 4.1 %collective-permute-done = f32[2,256,256]{1,2,0:T(8,128)} collective-permute-done((f32[2,256,256]{1,2,0:T(8,128)S(1)}, f32[2,256,256]{1,2,0:T(8,128)}, u32[]{:S(2)}, u32[]{:S(2)}) %collective-permute-start) | collective-permute-done | bytes 524320 | tf_op jit(solution)/shard_map/ppermute | solution.py:35
  21.0 3.6 %collective-permute-start.7 = (f32[2,256,256]{1,2,0:T(8,128)S(1)}, f32[2,256,256]{1,2,0:T(8,128)S(1)}, u32[]{:S(2)}, u32[]{:S(2)}) collective-permute-start(f32[2,256,256]{1,2,0:T(8,128)S(1)} %bitcast.129), channel_id=1, source_target_pairs={{0,1},{1,2},{2,3},{3,0},{4,5},{5,6},{6,7},{7,4},{8,9},{9,10},{10,1... | collective-permute-start | bytes 1572872 | tf_op jit(solution)/shard_map/ppermute | solution.py:23
  27.5 3.5 %fusion.5 = f32[2,256,256]{1,2,0:T(8,128)S(1)} fusion(f32[2,256,256]{1,2,0:T(8,128)S(1)} %bitcast.134, f32[2,256,256]{1,2,0:T(8,128)S(1)} %copy-done.4, f32[2,256,256]{1,2,0:T(8,128)} %collective-permute-done.6, f32[2,256,256]{1,2,0:T(8,128)} %collective-permute-done.5, f32[1,3,2,256,256]{4,3,2,1,0:T(8,128)S(1)} %copy-done), kind=kOutput, calls=%fused_computation.17 | convolution fusion | flops 406257664 | bytes 3145728 | tf_op jit(solution)/shard_map/xyk,kz->xyz/dot_general | solution.py:54
  31.3 3.9 %fusion.2 = f32[2,256,256]{1,2,0:T(8,128)S(1)} fusion(f32[2,256,256]{1,2,0:T(8,128)} %bitcast.3, f32[2,256,256]{1,2,0:T(8,128)S(1)} %copy-done.3, f32[2,256,256]{1,2,0:T(8,128)} %collective-permute-done.4, f32[2,256,256]{1,2,0:T(8,128)} %collective-permute-done.3, f32[1,3,2,256,256]{4,3,2,1,0:T(8,128)S(1)} %copy-done), kind=kOutput, calls=%fused_computation.14 | convolution fusion | flops 406257664 | bytes 3145728 | tf_op jit(solution)/shard_map/xyk,kz->xyz/dot_general | solution.py:54
  36.8 10.8 %collective-permute-done.1 = f32[2,256,256]{1,2,0:T(8,128)S(1)} collective-permute-done((f32[2,256,256]{1,2,0:T(8,128)S(1)}, f32[2,256,256]{1,2,0:T(8,128)S(1)}, u32[]{:S(2)}, u32[]{:S(2)}) %collective-permute-start.1) | collective-permute-done | bytes 524320 | tf_op jit(solution)/shard_map/ppermute | solution.py:23
  47.5 3.0 %collective-permute-done.2 = f32[2,256,256]{1,2,0:T(8,128)S(1)} collective-permute-done((f32[2,256,256]{1,2,0:T(8,128)S(1)}, f32[2,256,256]{1,2,0:T(8,128)S(1)}, u32[]{:S(2)}, u32[]{:S(2)}) %collective-permute-start.2) | collective-permute-done | bytes 524320 | tf_op jit(solution)/shard_map/ppermute | solution.py:25
  50.6 1.9 %fusion.11 = f32[2,256,256]{1,2,0:T(8,128)S(1)} fusion(f32[2,256,256]{1,2,0:T(8,128)S(1)} %broadcast_select_fusion.1, f32[2,256,256]{1,2,0:T(8,128)S(1)} %convolution_bitcast_fusion.10, f32[2,256,256]{1,2,0:T(8,128)S(1)} %collective-permute-done.2, f32[2,256,256]{1,2,0:T(8,128)S(1)} %collective-permute-done.1), kind=kOutput, calls=%fused_computation.32 | convolution fusion | flops 406257664 | bytes 2621440 | tf_op jit(solution)/shard_map/xyk,kz->xyz/dot_general | solution.py:54
  52.5 2.3 %multiply_add_fusion.1 = (f32[2,256,256]{1,2,0:T(8,128)S(1)}, f32[2,256,256]{1,2,0:T(8,128)S(1)}) fusion(f32[2,256,256]{1,2,0:T(8,128)S(1)} %fusion.2, f32[2,256,256]{1,2,0:T(8,128)S(1)} %broadcast_select_fusion.1, f32[2,256,256]{1,2,0:T(8,128)S(1)} %fusion.11, f32[2,256,256]{1,2,0:T(8,128)S(1)} %fusion.5, f32[2,256,256]{1,2,0:T(8,128)S(1)} %bitcast.131, ...), kind=kOutput, calls=%fused_computation.124 | convolution fusion | flops 407568384 | bytes 5767168 | tf_op jit(solution)/shard_map/xyk,kz->xyz/dot_general | solution.py:54
  58.3 11.0 %collective-permute-done.10 = f32[2,256,256]{1,2,0:T(8,128)S(1)} collective-permute-done((f32[2,256,256]{1,2,0:T(8,128)S(1)}, f32[2,256,256]{1,2,0:T(8,128)S(1)}, u32[]{:S(2)}, u32[]{:S(2)}) %collective-permute-start.10) | collective-permute-done | bytes 524320 | tf_op jit(solution)/shard_map/ppermute | solution.py:25
  69.3 2.1 %multiply_add_fusion = (f32[2,256,256]{1,2,0:T(8,128)S(1)}, f32[2,256,256]{1,2,0:T(8,128)S(1)}) fusion(f32[2,256,256]{1,2,0:T(8,128)S(1)} %get-tuple-element.9, f32[2,256,256]{1,2,0:T(8,128)S(1)} %fusion.2, f32[2,256,256]{1,2,0:T(8,128)S(1)} %get-tuple-element.8, f32[2,256,256]{1,2,0:T(8,128)S(1)} %fusion.5, ...), kind=kOutput, calls=%fused_computation.123 | convolution fusion | flops 407568384 | bytes 4718592 | tf_op jit(solution)/shard_map/xyk,kz->xyz/dot_general | solution.py:54
  71.4 3.1 %collective-permute-start.11 = (f32[2,256,256]{1,2,0:T(8,128)S(1)}, f32[2,256,256]{1,2,0:T(8,128)S(1)}, u32[]{:S(2)}, u32[]{:S(2)}) collective-permute-start(f32[2,256,256]{1,2,0:T(8,128)S(1)} %get-tuple-element.10), channel_id=1, source_target_pairs={{0,4},{4,8},{8,12},{12,16},{16,20},{20,24},{24,28},{1,5},{5,9},{9,... | collective-permute-start | bytes 1572872 | tf_op jit(solution)/shard_map/ppermute | solution.py:35
  77.1 10.2 %collective-permute-done.11 = f32[2,256,256]{1,2,0:T(8,128)S(1)} collective-permute-done((f32[2,256,256]{1,2,0:T(8,128)S(1)}, f32[2,256,256]{1,2,0:T(8,128)S(1)}, u32[]{:S(2)}, u32[]{:S(2)}) %collective-permute-start.11) | collective-permute-done | bytes 524320 | tf_op jit(solution)/shard_map/ppermute | solution.py:35
  90.3 1.9 %fusion.10 = f32[2,256,256]{1,2,0:T(8,128)S(1)} fusion(f32[2,256,256]{1,2,0:T(8,128)S(1)} %get-tuple-element.10, f32[2,256,256]{1,2,0:T(8,128)S(1)} %convolution_bitcast_fusion.1, f32[2,256,256]{1,2,0:T(8,128)S(1)} %collective-permute-done.15, f32[2,256,256]{1,2,0:T(8,128)S(1)} %collective-permute-done.14), kind=kOutput, calls=%fused_computation.23 | convolution fusion | flops 406257664 | bytes 2621440 | tf_op jit(solution)/shard_map/xyk,kz->xyz/dot_general | solution.py:54
  92.3 4.8 %collective-permute-done.12 = f32[2,256,256]{1,2,0:T(8,128)S(1)} collective-permute-done((f32[2,256,256]{1,2,0:T(8,128)S(1)}, f32[2,256,256]{1,2,0:T(8,128)S(1)}, u32[]{:S(2)}, u32[]{:S(2)}) %collective-permute-start.12) | collective-permute-done | bytes 524320 | tf_op jit(solution)/shard_map/ppermute | solution.py:23
  97.1 5.4 %collective-permute-done.13 = f32[2,256,256]{1,2,0:T(8,128)S(1)} collective-permute-done((f32[2,256,256]{1,2,0:T(8,128)S(1)}, f32[2,256,256]{1,2,0:T(8,128)S(1)}, u32[]{:S(2)}, u32[]{:S(2)}) %collective-permute-start.13) | collective-permute-done | bytes 524320 | tf_op jit(solution)/shard_map/ppermute | solution.py:25
  102.5 2.1 %fusion.17 = f32[2,256,256]{1,2,0:T(8,128)S(1)} fusion(f32[2,256,256]{1,2,0:T(8,128)S(1)} %broadcast_select_fusion, f32[2,256,256]{1,2,0:T(8,128)S(1)} %fusion.11, f32[2,256,256]{1,2,0:T(8,128)S(1)} %convolution_bitcast_fusion.2, f32[2,256,256]{1,2,0:T(8,128)S(1)} %collective-permute-done.13, f32[2,256,256]{1,2,0:T(8,128)S(1)} %collective-permute-done.12, ...), kind=kOutput, calls=%fused_computation.38 | convolution fusion | flops 407568384 | bytes 4194304 | tf_op jit(solution)/shard_map/xyk,kz->xyz/dot_general | solution.py:54
  106.9 7.1 %collective-permute-done.16 = f32[2,256,256]{1,2,0:T(8,128)S(1)} collective-permute-done((f32[2,256,256]{1,2,0:T(8,128)S(1)}, f32[2,256,256]{1,2,0:T(8,128)S(1)}, u32[]{:S(2)}, u32[]{:S(2)}) %collective-permute-start.16) | collective-permute-done | bytes 524320 | tf_op jit(solution)/shard_map/ppermute | solution.py:23
  114.0 4.5 %collective-permute-done.17 = f32[2,256,256]{1,2,0:T(8,128)S(1)} collective-permute-done((f32[2,256,256]{1,2,0:T(8,128)S(1)}, f32[2,256,256]{1,2,0:T(8,128)S(1)}, u32[]{:S(2)}, u32[]{:S(2)}) %collective-permute-start.17) | collective-permute-done | bytes 524320 | tf_op jit(solution)/shard_map/ppermute | solution.py:25
  118.5 2.1 %fusion.23 = f32[1,2,256,256]{2,3,1,0:T(8,128)S(1)} fusion(f32[2,256,256]{1,2,0:T(8,128)S(1)} %fusion.17, f32[2,256,256]{1,2,0:T(8,128)S(1)} %get-tuple-element.11, f32[2,256,256]{1,2,0:T(8,128)S(1)} %convolution_bitcast_fusion, f32[2,256,256]{1,2,0:T(8,128)S(1)} %collective-permute-done.17, f32[2,256,256]{1,2,0:T(8,128)S(1)} %collective-permute-done.16, ...), kind=kOutput, calls=%fused_computation.44 | convolution fusion | flops 407568384 | bytes 4194304 | tf_op jit(solution)/shard_map/xyk,kz->xyz/dot_general | solution.py:54
  (47 shorter events, 22.6 us)
Async XLA Ops:
  1.5 7.9 %copy-start = (f32[1,3,2,256,256]{4,3,2,1,0:T(8,128)S(1)}, f32[1,3,2,256,256]{4,3,2,1,0:T(8,128)}, u32[]{:S(2)}) copy-start(f32[1,3,2,256,256]{4,3,2,1,0:T(8,128)} %param.3) | copy-start | bytes 4718596
  2.5 23.2 %collective-permute-start.5 = (f32[2,256,256]{1,2,0:T(8,128)}, f32[2,256,256]{1,2,0:T(8,128)}, u32[]{:S(2)}, u32[]{:S(2)}) collective-permute-start(f32[2,256,256]{1,2,0:T(8,128)} %bitcast.132), channel_id=1, source_target_pairs={{0,1},{1,2},{2,3},{3,0},{4,5},{5,6},{6,7},{7,4},{8,9},{9,10},{10,1... | collective-permute-start | bytes 1572872 | tf_op jit(solution)/shard_map/ppermute | solution.py:23
  3.3 22.5 %collective-permute-start.6 = (f32[2,256,256]{1,2,0:T(8,128)}, f32[2,256,256]{1,2,0:T(8,128)}, u32[]{:S(2)}, u32[]{:S(2)}) collective-permute-start(f32[2,256,256]{1,2,0:T(8,128)} %bitcast.133), channel_id=1, source_target_pairs={{1,0},{2,1},{3,2},{0,3},{5,4},{6,5},{7,6},{4,7},{9,8},{10,9},{11,1... | collective-permute-start | bytes 1572872 | tf_op jit(solution)/shard_map/ppermute | solution.py:25
  4.3 26.8 %collective-permute-start.3 = (f32[2,256,256]{1,2,0:T(8,128)}, f32[2,256,256]{1,2,0:T(8,128)}, u32[]{:S(2)}, u32[]{:S(2)}) collective-permute-start(f32[2,256,256]{1,2,0:T(8,128)} %bitcast.3), channel_id=1, source_target_pairs={{0,1},{1,2},{2,3},{3,0},{4,5},{5,6},{6,7},{7,4},{8,9},{9,10},{10,1... | collective-permute-start | bytes 1572872 | tf_op jit(solution)/shard_map/ppermute | solution.py:23
  6.0 25.3 %collective-permute-start.4 = (f32[2,256,256]{1,2,0:T(8,128)}, f32[2,256,256]{1,2,0:T(8,128)}, u32[]{:S(2)}, u32[]{:S(2)}) collective-permute-start(f32[2,256,256]{1,2,0:T(8,128)} %bitcast.3), channel_id=1, source_target_pairs={{1,0},{2,1},{3,2},{0,3},{5,4},{6,5},{7,6},{4,7},{9,8},{10,9},{11,1... | collective-permute-start | bytes 1572872 | tf_op jit(solution)/shard_map/ppermute | solution.py:25
  6.2 14.7 %collective-permute-start = (f32[2,256,256]{1,2,0:T(8,128)S(1)}, f32[2,256,256]{1,2,0:T(8,128)}, u32[]{:S(2)}, u32[]{:S(2)}) collective-permute-start(f32[2,256,256]{1,2,0:T(8,128)S(1)} %bitcast.128), channel_id=1, source_target_pairs={{0,4},{4,8},{8,12},{12,16},{16,20},{20,24},{24,28},{1,5},{5,9},{9,... | collective-permute-start | bytes 1572872 | tf_op jit(solution)/shard_map/ppermute | solution.py:35
  12.0 2.7 %copy-start.1 = (f32[2,256,256]{2,1,0:T(8,128)S(1)}, f32[2,256,256]{2,1,0:T(8,128)}, u32[]{:S(2)}) copy-start(f32[2,256,256]{2,1,0:T(8,128)} %param.2) | copy-start | bytes 1572868
  14.9 12.6 %copy-start.2 = (f32[1,1,2,256,256]{3,4,2,1,0:T(8,128)S(1)}, f32[1,1,2,256,256]{3,4,2,1,0:T(8,128)}, u32[]{:S(2)}) copy-start(f32[1,1,2,256,256]{3,4,2,1,0:T(8,128)} %copy.58) | copy-start | bytes 1572868
  14.9 12.6 %copy-start.4 = (f32[2,256,256]{1,2,0:T(8,128)S(1)}, f32[2,256,256]{1,2,0:T(8,128)}, u32[]{:S(2)}) copy-start(f32[2,256,256]{1,2,0:T(8,128)} %convolution_bitcast_fusion.7) | copy-start | bytes 1572868
  21.0 31.6 %collective-permute-start.7 = (f32[2,256,256]{1,2,0:T(8,128)S(1)}, f32[2,256,256]{1,2,0:T(8,128)S(1)}, u32[]{:S(2)}, u32[]{:S(2)}) collective-permute-start(f32[2,256,256]{1,2,0:T(8,128)S(1)} %bitcast.129), channel_id=1, source_target_pairs={{0,1},{1,2},{2,3},{3,0},{4,5},{5,6},{6,7},{7,4},{8,9},{9,10},{10,1... | collective-permute-start | bytes 1572872 | tf_op jit(solution)/shard_map/ppermute | solution.py:23
  25.7 5.6 %copy-start.3 = (f32[2,256,256]{1,2,0:T(8,128)S(1)}, f32[2,256,256]{1,2,0:T(8,128)}, u32[]{:S(2)}) copy-start(f32[2,256,256]{1,2,0:T(8,128)} %convolution_bitcast_fusion.9) | copy-start | bytes 1572868
  25.7 26.8 %collective-permute-start.8 = (f32[2,256,256]{1,2,0:T(8,128)S(1)}, f32[2,256,256]{1,2,0:T(8,128)S(1)}, u32[]{:S(2)}, u32[]{:S(2)}) collective-permute-start(f32[2,256,256]{1,2,0:T(8,128)S(1)} %bitcast.130), channel_id=1, source_target_pairs={{1,0},{2,1},{3,2},{0,3},{5,4},{6,5},{7,6},{4,7},{9,8},{10,9},{11,1... | collective-permute-start | bytes 1572872 | tf_op jit(solution)/shard_map/ppermute | solution.py:25
  25.8 21.8 %collective-permute-start.1 = (f32[2,256,256]{1,2,0:T(8,128)S(1)}, f32[2,256,256]{1,2,0:T(8,128)S(1)}, u32[]{:S(2)}, u32[]{:S(2)}) collective-permute-start(f32[2,256,256]{1,2,0:T(8,128)S(1)} %broadcast_select_fusion.1), channel_id=1, source_target_pairs={{0,1},{1,2},{2,3},{3,0},{4,5},{5,6},{6,7},{7,4},{8,9},{9,10},{10,1... | collective-permute-start | bytes 1572872 | tf_op jit(solution)/shard_map/ppermute | solution.py:23
  31.0 19.6 %collective-permute-start.2 = (f32[2,256,256]{1,2,0:T(8,128)S(1)}, f32[2,256,256]{1,2,0:T(8,128)S(1)}, u32[]{:S(2)}, u32[]{:S(2)}) collective-permute-start(f32[2,256,256]{1,2,0:T(8,128)S(1)} %broadcast_select_fusion.1), channel_id=1, source_target_pairs={{1,0},{2,1},{3,2},{0,3},{5,4},{6,5},{7,6},{4,7},{9,8},{10,9},{11,1... | collective-permute-start | bytes 1572872 | tf_op jit(solution)/shard_map/ppermute | solution.py:25
  54.9 14.4 %collective-permute-start.10 = (f32[2,256,256]{1,2,0:T(8,128)S(1)}, f32[2,256,256]{1,2,0:T(8,128)S(1)}, u32[]{:S(2)}, u32[]{:S(2)}) collective-permute-start(f32[2,256,256]{1,2,0:T(8,128)S(1)} %get-tuple-element.8), channel_id=1, source_target_pairs={{1,0},{2,1},{3,2},{0,3},{5,4},{6,5},{7,6},{4,7},{9,8},{10,9},{11,1... | collective-permute-start | bytes 1572872 | tf_op jit(solution)/shard_map/ppermute | solution.py:25
  54.9 14.4 %collective-permute-start.9 = (f32[2,256,256]{1,2,0:T(8,128)S(1)}, f32[2,256,256]{1,2,0:T(8,128)S(1)}, u32[]{:S(2)}, u32[]{:S(2)}) collective-permute-start(f32[2,256,256]{1,2,0:T(8,128)S(1)} %get-tuple-element.8), channel_id=1, source_target_pairs={{0,1},{1,2},{2,3},{3,0},{4,5},{5,6},{6,7},{7,4},{8,9},{9,10},{10,1... | collective-permute-start | bytes 1572872 | tf_op jit(solution)/shard_map/ppermute | solution.py:23
  71.4 15.9 %collective-permute-start.11 = (f32[2,256,256]{1,2,0:T(8,128)S(1)}, f32[2,256,256]{1,2,0:T(8,128)S(1)}, u32[]{:S(2)}, u32[]{:S(2)}) collective-permute-start(f32[2,256,256]{1,2,0:T(8,128)S(1)} %get-tuple-element.10), channel_id=1, source_target_pairs={{0,4},{4,8},{8,12},{12,16},{16,20},{20,24},{24,28},{1,5},{5,9},{9,... | collective-permute-start | bytes 1572872 | tf_op jit(solution)/shard_map/ppermute | solution.py:35
  74.5 15.8 %collective-permute-start.14 = (f32[2,256,256]{1,2,0:T(8,128)S(1)}, f32[2,256,256]{1,2,0:T(8,128)S(1)}, u32[]{:S(2)}, u32[]{:S(2)}) collective-permute-start(f32[2,256,256]{1,2,0:T(8,128)S(1)} %get-tuple-element.10), channel_id=1, source_target_pairs={{0,1},{1,2},{2,3},{3,0},{4,5},{5,6},{6,7},{7,4},{8,9},{9,10},{10,1... | collective-permute-start | bytes 1572872 | tf_op jit(solution)/shard_map/ppermute | solution.py:23
  75.5 14.9 %collective-permute-start.15 = (f32[2,256,256]{1,2,0:T(8,128)S(1)}, f32[2,256,256]{1,2,0:T(8,128)S(1)}, u32[]{:S(2)}, u32[]{:S(2)}) collective-permute-start(f32[2,256,256]{1,2,0:T(8,128)S(1)} %get-tuple-element.10), channel_id=1, source_target_pairs={{1,0},{2,1},{3,2},{0,3},{5,4},{6,5},{7,6},{4,7},{9,8},{10,9},{11,1... | collective-permute-start | bytes 1572872 | tf_op jit(solution)/shard_map/ppermute | solution.py:25
  87.3 9.7 %collective-permute-start.12 = (f32[2,256,256]{1,2,0:T(8,128)S(1)}, f32[2,256,256]{1,2,0:T(8,128)S(1)}, u32[]{:S(2)}, u32[]{:S(2)}) collective-permute-start(f32[2,256,256]{1,2,0:T(8,128)S(1)} %broadcast_select_fusion), channel_id=1, source_target_pairs={{0,1},{1,2},{2,3},{3,0},{4,5},{5,6},{6,7},{7,4},{8,9},{9,10},{10,1... | collective-permute-start | bytes 1572872 | tf_op jit(solution)/shard_map/ppermute | solution.py:23
  87.9 14.5 %collective-permute-start.13 = (f32[2,256,256]{1,2,0:T(8,128)S(1)}, f32[2,256,256]{1,2,0:T(8,128)S(1)}, u32[]{:S(2)}, u32[]{:S(2)}) collective-permute-start(f32[2,256,256]{1,2,0:T(8,128)S(1)} %broadcast_select_fusion), channel_id=1, source_target_pairs={{1,0},{2,1},{3,2},{0,3},{5,4},{6,5},{7,6},{4,7},{9,8},{10,9},{11,1... | collective-permute-start | bytes 1572872 | tf_op jit(solution)/shard_map/ppermute | solution.py:25
  104.5 9.5 %collective-permute-start.16 = (f32[2,256,256]{1,2,0:T(8,128)S(1)}, f32[2,256,256]{1,2,0:T(8,128)S(1)}, u32[]{:S(2)}, u32[]{:S(2)}) collective-permute-start(f32[2,256,256]{1,2,0:T(8,128)S(1)} %fusion.17), channel_id=1, source_target_pairs={{0,1},{1,2},{2,3},{3,0},{4,5},{5,6},{6,7},{7,4},{8,9},{9,10},{10,1... | collective-permute-start | bytes 1572872 | tf_op jit(solution)/shard_map/ppermute | solution.py:23
  104.6 13.9 %collective-permute-start.17 = (f32[2,256,256]{1,2,0:T(8,128)S(1)}, f32[2,256,256]{1,2,0:T(8,128)S(1)}, u32[]{:S(2)}, u32[]{:S(2)}) collective-permute-start(f32[2,256,256]{1,2,0:T(8,128)S(1)} %fusion.17), channel_id=1, source_target_pairs={{1,0},{2,1},{3,2},{0,3},{5,4},{6,5},{7,6},{4,7},{9,8},{10,9},{11,1... | collective-permute-start | bytes 1572872 | tf_op jit(solution)/shard_map/ppermute | solution.py:25
where the time goes:
time: 123 us; the launch traced here: 122 us
  waiting for transfers between devices  60.9 us (50%)
  matrix products  35 us (28%)
  starting transfers between devices  19.3 us (16%)
  local copies, waits for them, and re-layouts  5.48 us (4%)
  other arithmetic  1.28 us (1%)
    ppermute x8, waiting for transfers between devices, padded_2(): lax.ppermute(head, axis, [((i + 1) % count, i) for i in range(count)])  24 us
    ppermute x8, waiting for transfers between devices, padded_2(): lax.ppermute(tail, axis, [(i, (i + 1) % count) for i in range(count)])  22.6 us
    dot_general x8, matrix products, evaluate(): jnp.einsum('xyk,kz->xyz', state_field, matrix_z, precision=lax.Precision....  19.7 us
    dot_general x8, matrix products, evaluate(): jnp.einsum('jk,xkz->xjz', matrix_y, state_field, precision=lax.Precision....  15.3 us
    ppermute x2, waiting for transfers between devices, passed_along(): return lax.ppermute(shard, axis, pairs)  14.3 us
    ppermute x8, starting transfers between devices, padded_2(): lax.ppermute(tail, axis, [(i, (i + 1) % count) for i in range(count)])  11.2 us
    ppermute x2, starting transfers between devices, passed_along(): return lax.ppermute(shard, axis, pairs)  6.24 us
  transfers between devices with their start and end apart: 18, of which 9 were waited for; matrix products, arithmetic and copies ran while one was open for 24% of the time, Pallas kernels for 0%

commit v1 on v0

v1 whole, which is shorter than its diff:
```python
import math

import jax
import jax.numpy as jnp
from jax import lax
from jax.sharding import PartitionSpec as P

SWEEPS = 2
CHUNKS = 2

spacing = 2.0
step_size = 0.2
half_step = 0.1

MIDDLE = (
    step_size * 5.0 / 24.0 - half_step,
    step_size / 3.0,
    -step_size / 24.0,
)
FINAL = (
    -step_size / 24.0,
    step_size / 3.0 - half_step,
    step_size * 5.0 / 24.0,
)


def second_derivative(count):
    positions = jnp.arange(count, dtype=jnp.int32)
    offset = positions[None, :] - positions[:, None]
    angle_step = 2.0 * math.pi / count
    parity = jnp.where(offset % 2 == 0, 1.0, -1.0).astype(jnp.float32)
    safe = jnp.where(offset == 0, 1, offset).astype(jnp.float32)
    sine_value = jnp.sin(safe * (angle_step / 2.0))
    off_value = -0.5 * parity / (sine_value * sine_value)
    diagonal_value = -math.pi**2 / (3.0 * angle_step * angle_step) - 1.0 / 6.0
    matrix = jnp.where(offset == 0, jnp.float32(diagonal_value), off_value)
    return matrix * (angle_step / spacing) ** 2


def relayed(shard):
    length = lax.axis_size("tm")
    return lax.ppermute(shard, "tm", [(i, i + 1) for i in range(length - 1)])


def neighbours(part):
    count = lax.axis_size("gx")
    head, tail = part[:2], part[part.shape[0] - 2 :]
    if count % 2:
        left = lax.ppermute(tail, "gx", [(i, (i + 1) % count) for i in range(count)])
        right = lax.ppermute(head, "gx", [((i + 1) % count, i) for i in range(count)])
        return left, right
    even = lax.axis_index("gx") % 2 == 0
    inner, outer = [], []
    for i in range(0, count, 2):
        inner += [(i, i + 1), (i + 1, i)]
        outer += [(i + 1, (i + 2) % count), ((i + 2) % count, i + 1)]
    if part.shape[0] == 2:
        to_inner = to_outer = part
    else:
        to_inner = jnp.where(even, tail, head)
        to_outer = jnp.where(even, head, tail)
    across = lax.ppermute(to_outer, "gx", outer)
    beside = lax.ppermute(to_inner, "gx", inner)
    return jnp.where(even, across, beside), jnp.where(even, beside, across)


def stencil(part, left, right):
    planes = [left[0], left[1], *part, right[0], right[1]]
    rows = []
    for i in range(2, len(planes) - 2):
        near = planes[i - 1] + planes[i + 1]
        far = planes[i - 2] + planes[i + 2]
        rows.append((16.0 * near - far - 18.0 * planes[i]) * (1.0 / 12.0))
    return jnp.stack(rows)


def products(field, matrix_y, matrix_z):
    term_y = jnp.einsum("jk,xkz->xjz", matrix_y, field, precision=lax.Precision.HIGH)
    term_z = jnp.einsum("xyk,kz->xyz", field, matrix_z, precision=lax.Precision.HIGH)
    return term_y + term_z


def weighted(weights, parts):
    return sum(w * p for w, p in zip(weights, parts))


def advance(base, drive, matrix_y, matrix_z):
    halos = [neighbours(part) for part in drive]
    whole = products(jnp.concatenate(drive, axis=1), matrix_y, matrix_z)
    terms = jnp.split(whole, len(drive), axis=1)
    return [b + (t + stencil(d, *h)) for b, t, d, h in zip(base, terms, drive, halos)]


def local(initial, node_values):
    matrix_y = second_derivative(node_values.shape[3])
    matrix_z = second_derivative(node_values.shape[4])
    leading = lax.axis_index("tm") == 0
    cut = lambda item: jnp.split(item, CHUNKS, axis=1)
    start = cut(initial)
    values = [cut(node_values[0, m]) for m in range(3)]
    for _ in range(SWEEPS):
        old = list(zip(*values))
        linear_one = [weighted(MIDDLE, u) for u in old]
        linear_two = [weighted(FINAL, u) for u in old]
        cubic_one = [weighted(MIDDLE, [x * x * x for x in u]) for u in old]
        cubic_two = [weighted(FINAL, [x * x * x for x in u]) for u in old]
        first = [jnp.where(leading, s, relayed(u[2])) for s, u in zip(start, old)]
        drive = [half_step * a + w for a, w in zip(first, linear_one)]
        base = [a - half_step * a * a * a - c for a, c in zip(first, cubic_one)]
        middle = advance(base, drive, matrix_y, matrix_z)
        drive = [half_step * a + w for a, w in zip(middle, linear_two)]
        base = [a - half_step * a * a * a - c for a, c in zip(middle, cubic_two)]
        final = advance(base, drive, matrix_y, matrix_z)
        values = [first, middle, final]
    return jnp.stack([jnp.concatenate(v, axis=1) for v in values])[None]


def solution(mesh):
    in_specs = (P("gx", None, None), P("tm", None, "gx", None, None))
    out_specs = P("tm", None, "gx", None, None)
    return jax.shard_map(local, mesh=mesh, in_specs=in_specs, out_specs=out_specs, check_vma=False)
```

time: 123 us -> 95.6 us (0.78)
  matrix products: 35 us -> 11.2 us
  local copies, waits for them, and re-layouts: 5.48 us -> 1.56 us
  waiting for transfers between devices: 60.9 us -> 57.5 us
  other arithmetic: 1.28 us -> 4.22 us
  starting transfers between devices: 19.3 us -> 20.6 us
    dot_general x16 -> x8, matrix products: 35 us -> 11.2 us  [the longest x4 5.62 us: products(): jnp.einsum('jk,xkz->xjz', matrix_y, field, precision=lax.Precision.HIGH)]
    ppermute x18 -> x20, waiting for transfers between devices: 60.9 us -> 57.5 us  [the longest x8 35.4 us: neighbours(): across = lax.ppermute(to_outer, 'gx', outer)]
    unnamed x14 -> x2, local copies, waits for them, and re-layouts: 2.4 us -> 0.01 us
    add x0 -> x6, other arithmetic: none -> 1.91 us  [the longest x2 0.87 us: local(): drive = [half_step * a + w for a, w in zip(middle, linear_two)]]
    broadcast_in_dim x1 -> x0, local copies, waits for them, and re-layouts: 1.61 us -> none  [local(): return jnp.stack(values, axis=0)[None]]
    squeeze x0 -> x1, local copies, waits for them, and re-layouts: none -> 1.52 us  [local(): values = [cut(node_values[0, m]) for m in range(3)]]
    slice x1 -> x0, local copies, waits for them, and re-layouts: 1.46 us -> none  [local(): values = [node_values[0, 0], node_values[0, 1], node_values[0, 2]]]
    ppermute x18 -> x20, starting transfers between devices: 19.3 us -> 20.6 us  [the longest x4 9.36 us: relayed(): return lax.ppermute(shard, 'tm', [(i, i + 1) for i in range(length - 1)])]
  transfers between devices with their start and end apart: 18 -> 20, of which waited for: 9 -> 12; matrix products, arithmetic and copies ran while one was open for 24% -> 12% of each run, Pallas kernels for 0% -> 0%
where the time goes in v1:
time: 95.6 us; the launch traced here: 95.3 us
  waiting for transfers between devices  57.5 us (60%)
  starting transfers between devices  20.6 us (22%)
  matrix products  11.2 us (12%)
  other arithmetic  4.22 us (4%)
  local copies, waits for them, and re-layouts  1.56 us (2%)
    ppermute x8, waiting for transfers between devices, neighbours(): across = lax.ppermute(to_outer, 'gx', outer)  35.4 us
    ppermute x4, waiting for transfers between devices, relayed(): return lax.ppermute(shard, 'tm', [(i, i + 1) for i in range(length - 1)])  22.1 us
    ppermute x4, starting transfers between devices, relayed(): return lax.ppermute(shard, 'tm', [(i, i + 1) for i in range(length - 1)])  9.36 us
    ppermute x8, starting transfers between devices, neighbours(): across = lax.ppermute(to_outer, 'gx', outer)  6.99 us
    dot_general x4, matrix products, products(): jnp.einsum('jk,xkz->xjz', matrix_y, field, precision=lax.Precision.HIGH)  5.62 us
    dot_general x4, matrix products, products(): jnp.einsum('xyk,kz->xyz', field, matrix_z, precision=lax.Precision.HIGH)  5.58 us
    ppermute x8, starting transfers between devices, neighbours(): beside = lax.ppermute(to_inner, 'gx', inner)  4.21 us
  transfers between devices with their start and end apart: 20, of which 12 were waited for; matrix products, arithmetic and copies ran while one was open for 12% of the time, Pallas kernels for 0%

profile of v1, /device:TPU:29, one launch (start us, length us, event | category | flops | bytes accessed | tf_op | source)
XLA Modules:
  0.0 95.3 jit_solution(1695174921972715838)
XLA Ops:
  0.0 1.5 %slice_bitcast_fusion.2 = (f32[2,256,256]{2,1,0:T(8,128)S(1)}, f32[2,256,256]{2,1,0:T(8,128)S(1)}, f32[2,256,256]{2,1,0:T(8,128)S(1)}) fusion(f32[1,3,2,256,256]{4,3,2,1,0:T(8,128)} %param.3), kind=kLoop, calls=%fused_computation.18 | loop fusion | bytes 3145728 | tf_op jit(solution)/shard_map/squeeze | solution.py:100
  1.6 3.1 %collective-permute-start = (f32[2,128,256]{2,1,0:T(8,128)S(1)}, f32[2,128,256]{2,1,0:T(8,128)S(1)}, u32[]{:S(2)}, u32[]{:S(2)}) collective-permute-start(f32[2,128,256]{2,1,0:T(8,128)S(1)} %get-tuple-element.66), channel_id=1, source_target_pairs={{0,4},{4,8},{8,12},{12,16},{16,20},{20,24},{24,28},{1,5},{5,9},{9,... | collective-permute-start | bytes 786440 | tf_op jit(solution)/shard_map/ppermute | solution.py:42
  4.7 1.9 %collective-permute-start.1 = (f32[2,128,256]{2,1,0:T(8,128)S(1)}, f32[2,128,256]{2,1,0:T(8,128)S(1)}, u32[]{:S(2)}, u32[]{:S(2)}) collective-permute-start(f32[2,128,256]{2,1,0:T(8,128)S(1)} %get-tuple-element.67), channel_id=1, source_target_pairs={{0,4},{4,8},{8,12},{12,16},{16,20},{20,24},{24,28},{1,5},{5,9},{9,... | collective-permute-start | bytes 786440 | tf_op jit(solution)/shard_map/ppermute | solution.py:42
  6.6 4.9 %collective-permute-done = f32[2,128,256]{2,1,0:T(8,128)S(1)} collective-permute-done((f32[2,128,256]{2,1,0:T(8,128)S(1)}, f32[2,128,256]{2,1,0:T(8,128)S(1)}, u32[]{:S(2)}, u32[]{:S(2)}) %collective-permute-start) | collective-permute-done | bytes 262176 | tf_op jit(solution)/shard_map/ppermute | solution.py:42
  11.6 5.6 %collective-permute-done.1 = f32[2,128,256]{2,1,0:T(8,128)S(1)} collective-permute-done((f32[2,128,256]{2,1,0:T(8,128)S(1)}, f32[2,128,256]{2,1,0:T(8,128)S(1)}, u32[]{:S(2)}, u32[]{:S(2)}) %collective-permute-start.1) | collective-permute-done | bytes 262176 | tf_op jit(solution)/shard_map/ppermute | solution.py:42
  17.4 1.6 %collective-permute-start.3 = (f32[2,128,256]{2,1,0:T(8,128)S(1)}, f32[2,128,256]{2,1,0:T(8,128)S(1)}, u32[]{:S(2)}, u32[]{:S(2)}) collective-permute-start(f32[2,128,256]{2,1,0:T(8,128)S(1)} %get-tuple-element.17), channel_id=1, source_target_pairs={{0,1},{1,0},{2,3},{3,2},{4,5},{5,4},{6,7},{7,6},{8,9},{9,8},{10,11... | collective-permute-start | bytes 786440 | tf_op jit(solution)/shard_map/ppermute | solution.py:63
  22.2 1.4 %fusion = f32[2,256,256]{2,1,0:T(8,128)S(1)} fusion(f32[2,256,256]{2,1,0:T(8,128)S(1)} %fusion.7, f32[2,128,256]{2,1,0:T(8,128)S(1)} %get-tuple-element.25, f32[2,128,256]{2,1,0:T(8,128)S(1)} %get-tuple-element.17), kind=kOutput, calls=%fused_computation.5 | convolution fusion | flops 203096064 | bytes 1572864 | tf_op jit(solution)/shard_map/jk,xkz->xjz/dot_general | solution.py:78
  23.6 4.2 %collective-permute-done.2 = f32[2,128,256]{2,1,0:T(8,128)S(1)} collective-permute-done((f32[2,128,256]{2,1,0:T(8,128)S(1)}, f32[2,128,256]{2,1,0:T(8,128)S(1)}, u32[]{:S(2)}, u32[]{:S(2)}) %collective-permute-start.2) | collective-permute-done | bytes 262176 | tf_op jit(solution)/shard_map/ppermute | solution.py:62
  28.0 4.6 %collective-permute-done.4 = f32[2,128,256]{2,1,0:T(8,128)S(1)} collective-permute-done((f32[2,128,256]{2,1,0:T(8,128)S(1)}, f32[2,128,256]{2,1,0:T(8,128)S(1)}, u32[]{:S(2)}, u32[]{:S(2)}) %collective-permute-start.4) | collective-permute-done | bytes 262176 | tf_op jit(solution)/shard_map/ppermute | solution.py:62
  33.9 1.6 %collective-permute-start.9 = (f32[2,128,256]{2,1,0:T(8,128)S(1)}, f32[2,128,256]{2,1,0:T(8,128)S(1)}, u32[]{:S(2)}, u32[]{:S(2)}) collective-permute-start(f32[2,128,256]{2,1,0:T(8,128)S(1)} %get-tuple-element.23), channel_id=1, source_target_pairs={{1,2},{2,1},{3,0},{0,3},{5,6},{6,5},{7,4},{4,7},{9,10},{10,9},{11,... | collective-permute-start | bytes 786440 | tf_op jit(solution)/shard_map/ppermute | solution.py:62
  35.5 1.4 %fusion.6 = f32[2,256,256]{2,1,0:T(8,128)S(1)} fusion(f32[2,128,256]{2,1,0:T(8,128)S(1)} %get-tuple-element.23, f32[2,128,256]{2,1,0:T(8,128)S(1)} %get-tuple-element.13), kind=kOutput, calls=%fused_computation.21 | convolution fusion | flops 202964992 | bytes 1048576 | tf_op jit(solution)/shard_map/xyk,kz->xyz/dot_general | solution.py:79
  36.9 1.4 %fusion.1 = f32[2,256,256]{2,1,0:T(8,128)S(1)} fusion(f32[2,256,256]{2,1,0:T(8,128)S(1)} %fusion.6, f32[2,128,256]{2,1,0:T(8,128)S(1)} %get-tuple-element.23, f32[2,128,256]{2,1,0:T(8,128)S(1)} %get-tuple-element.13), kind=kOutput, calls=%fused_computation.6 | convolution fusion | flops 203096064 | bytes 1572864 | tf_op jit(solution)/shard_map/jk,xkz->xjz/dot_general | solution.py:78
  38.3 3.9 %collective-permute-done.6 = f32[2,128,256]{2,1,0:T(8,128)S(1)} collective-permute-done((f32[2,128,256]{2,1,0:T(8,128)S(1)}, f32[2,128,256]{2,1,0:T(8,128)S(1)}, u32[]{:S(2)}, u32[]{:S(2)}) %collective-permute-start.6) | collective-permute-done | bytes 262176 | tf_op jit(solution)/shard_map/ppermute | solution.py:62
  42.4 4.9 %collective-permute-done.9 = f32[2,128,256]{2,1,0:T(8,128)S(1)} collective-permute-done((f32[2,128,256]{2,1,0:T(8,128)S(1)}, f32[2,128,256]{2,1,0:T(8,128)S(1)}, u32[]{:S(2)}, u32[]{:S(2)}) %collective-permute-start.9) | collective-permute-done | bytes 262176 | tf_op jit(solution)/shard_map/ppermute | solution.py:62
  47.8 2.2 %collective-permute-start.8 = (f32[2,128,256]{2,1,0:T(8,128)S(1)}, f32[2,128,256]{2,1,0:T(8,128)S(1)}, u32[]{:S(2)}, u32[]{:S(2)}) collective-permute-start(f32[2,128,256]{2,1,0:T(8,128)S(1)} %get-tuple-element.21), channel_id=1, source_target_pairs={{0,4},{4,8},{8,12},{12,16},{16,20},{20,24},{24,28},{1,5},{5,9},{9,... | collective-permute-start | bytes 786440 | tf_op jit(solution)/shard_map/ppermute | solution.py:42
  50.0 2.1 %collective-permute-start.11 = (f32[2,128,256]{2,1,0:T(8,128)S(1)}, f32[2,128,256]{2,1,0:T(8,128)S(1)}, u32[]{:S(2)}, u32[]{:S(2)}) collective-permute-start(f32[2,128,256]{2,1,0:T(8,128)S(1)} %get-tuple-element.22), channel_id=1, source_target_pairs={{0,4},{4,8},{8,12},{12,16},{16,20},{20,24},{24,28},{1,5},{5,9},{9,... | collective-permute-start | bytes 786440 | tf_op jit(solution)/shard_map/ppermute | solution.py:42
  52.1 5.9 %collective-permute-done.8 = f32[2,128,256]{2,1,0:T(8,128)S(1)} collective-permute-done((f32[2,128,256]{2,1,0:T(8,128)S(1)}, f32[2,128,256]{2,1,0:T(8,128)S(1)}, u32[]{:S(2)}, u32[]{:S(2)}) %collective-permute-start.8) | collective-permute-done | bytes 262176 | tf_op jit(solution)/shard_map/ppermute | solution.py:42
  58.0 5.6 %collective-permute-done.11 = f32[2,128,256]{2,1,0:T(8,128)S(1)} collective-permute-done((f32[2,128,256]{2,1,0:T(8,128)S(1)}, f32[2,128,256]{2,1,0:T(8,128)S(1)}, u32[]{:S(2)}, u32[]{:S(2)}) %collective-permute-start.11) | collective-permute-done | bytes 262176 | tf_op jit(solution)/shard_map/ppermute | solution.py:42
  69.9 4.2 %collective-permute-done.12 = f32[2,128,256]{2,1,0:T(8,128)S(1)} collective-permute-done((f32[2,128,256]{2,1,0:T(8,128)S(1)}, f32[2,128,256]{2,1,0:T(8,128)S(1)}, u32[]{:S(2)}, u32[]{:S(2)}) %collective-permute-start.12) | collective-permute-done | bytes 262176 | tf_op jit(solution)/shard_map/ppermute | solution.py:62
  74.2 4.6 %collective-permute-done.14 = f32[2,128,256]{2,1,0:T(8,128)S(1)} collective-permute-done((f32[2,128,256]{2,1,0:T(8,128)S(1)}, f32[2,128,256]{2,1,0:T(8,128)S(1)}, u32[]{:S(2)}, u32[]{:S(2)}) %collective-permute-start.14) | collective-permute-done | bytes 262176 | tf_op jit(solution)/shard_map/ppermute | solution.py:62
  80.1 1.6 %collective-permute-start.18 = (f32[2,128,256]{2,1,0:T(8,128)S(1)}, f32[2,128,256]{2,1,0:T(8,128)S(1)}, u32[]{:S(2)}, u32[]{:S(2)}) collective-permute-start(f32[2,128,256]{2,1,0:T(8,128)S(1)} %get-tuple-element.52), channel_id=1, source_target_pairs={{1,2},{2,1},{3,0},{0,3},{5,6},{6,5},{7,4},{4,7},{9,10},{10,9},{11,... | collective-permute-start | bytes 786440 | tf_op jit(solution)/shard_map/ppermute | solution.py:62
  83.1 1.4 %fusion.3 = f32[2,256,256]{2,1,0:T(8,128)S(1)} fusion(f32[2,256,256]{2,1,0:T(8,128)S(1)} %fusion.4, f32[2,128,256]{2,1,0:T(8,128)S(1)} %get-tuple-element.52, f32[2,128,256]{2,1,0:T(8,128)S(1)} %get-tuple-element.5), kind=kOutput, calls=%fused_computation.8 | convolution fusion | flops 203096064 | bytes 1572864 | tf_op jit(solution)/shard_map/jk,xkz->xjz/dot_general | solution.py:78
  84.5 3.9 %collective-permute-done.16 = f32[2,128,256]{2,1,0:T(8,128)S(1)} collective-permute-done((f32[2,128,256]{2,1,0:T(8,128)S(1)}, f32[2,128,256]{2,1,0:T(8,128)S(1)}, u32[]{:S(2)}, u32[]{:S(2)}) %collective-permute-start.16) | collective-permute-done | bytes 262176 | tf_op jit(solution)/shard_map/ppermute | solution.py:62
  88.4 5.1 %collective-permute-done.18 = f32[2,128,256]{2,1,0:T(8,128)S(1)} collective-permute-done((f32[2,128,256]{2,1,0:T(8,128)S(1)}, f32[2,128,256]{2,1,0:T(8,128)S(1)}, u32[]{:S(2)}, u32[]{:S(2)}) %collective-permute-start.18) | collective-permute-done | bytes 262176 | tf_op jit(solution)/shard_map/ppermute | solution.py:62
  (53 shorter events, 16.4 us)
Async XLA Ops:
  0.0 17.2 %copy-start = (f32[2,256,256]{2,1,0:T(8,128)S(1)}, f32[2,256,256]{2,1,0:T(8,128)}, u32[]{:S(2)}) copy-start(f32[2,256,256]{2,1,0:T(8,128)} %param.2) | copy-start | bytes 1572868
  1.6 10.0 %collective-permute-start = (f32[2,128,256]{2,1,0:T(8,128)S(1)}, f32[2,128,256]{2,1,0:T(8,128)S(1)}, u32[]{:S(2)}, u32[]{:S(2)}) collective-permute-start(f32[2,128,256]{2,1,0:T(8,128)S(1)} %get-tuple-element.66), channel_id=1, source_target_pairs={{0,4},{4,8},{8,12},{12,16},{16,20},{20,24},{24,28},{1,5},{5,9},{9,... | collective-permute-start | bytes 786440 | tf_op jit(solution)/shard_map/ppermute | solution.py:42
  4.7 12.5 %collective-permute-start.1 = (f32[2,128,256]{2,1,0:T(8,128)S(1)}, f32[2,128,256]{2,1,0:T(8,128)S(1)}, u32[]{:S(2)}, u32[]{:S(2)}) collective-permute-start(f32[2,128,256]{2,1,0:T(8,128)S(1)} %get-tuple-element.67), channel_id=1, source_target_pairs={{0,4},{4,8},{8,12},{12,16},{16,20},{20,24},{24,28},{1,5},{5,9},{9,... | collective-permute-start | bytes 786440 | tf_op jit(solution)/shard_map/ppermute | solution.py:42
  17.4 6.2 %collective-permute-start.3 = (f32[2,128,256]{2,1,0:T(8,128)S(1)}, f32[2,128,256]{2,1,0:T(8,128)S(1)}, u32[]{:S(2)}, u32[]{:S(2)}) collective-permute-start(f32[2,128,256]{2,1,0:T(8,128)S(1)} %get-tuple-element.17), channel_id=1, source_target_pairs={{0,1},{1,0},{2,3},{3,2},{4,5},{5,4},{6,7},{7,6},{8,9},{9,8},{10,11... | collective-permute-start | bytes 786440 | tf_op jit(solution)/shard_map/ppermute | solution.py:63
  19.0 8.9 %collective-permute-start.2 = (f32[2,128,256]{2,1,0:T(8,128)S(1)}, f32[2,128,256]{2,1,0:T(8,128)S(1)}, u32[]{:S(2)}, u32[]{:S(2)}) collective-permute-start(f32[2,128,256]{2,1,0:T(8,128)S(1)} %get-tuple-element.17), channel_id=1, source_target_pairs={{1,2},{2,1},{3,0},{0,3},{5,6},{6,5},{7,4},{4,7},{9,10},{10,9},{11,... | collective-permute-start | bytes 786440 | tf_op jit(solution)/shard_map/ppermute | solution.py:62
  19.2 8.9 %collective-permute-start.5 = (f32[2,128,256]{2,1,0:T(8,128)S(1)}, f32[2,128,256]{2,1,0:T(8,128)S(1)}, u32[]{:S(2)}, u32[]{:S(2)}) collective-permute-start(f32[2,128,256]{2,1,0:T(8,128)S(1)} %get-tuple-element.25), channel_id=1, source_target_pairs={{0,1},{1,0},{2,3},{3,2},{4,5},{5,4},{6,7},{7,6},{8,9},{9,8},{10,11... | collective-permute-start | bytes 786440 | tf_op jit(solution)/shard_map/ppermute | solution.py:63
  19.6 13.0 %collective-permute-start.4 = (f32[2,128,256]{2,1,0:T(8,128)S(1)}, f32[2,128,256]{2,1,0:T(8,128)S(1)}, u32[]{:S(2)}, u32[]{:S(2)}) collective-permute-start(f32[2,128,256]{2,1,0:T(8,128)S(1)} %get-tuple-element.25), channel_id=1, source_target_pairs={{1,2},{2,1},{3,0},{0,3},{5,6},{6,5},{7,4},{4,7},{9,10},{10,9},{11,... | collective-permute-start | bytes 786440 | tf_op jit(solution)/shard_map/ppermute | solution.py:62
  33.2 5.2 %collective-permute-start.7 = (f32[2,128,256]{2,1,0:T(8,128)S(1)}, f32[2,128,256]{2,1,0:T(8,128)S(1)}, u32[]{:S(2)}, u32[]{:S(2)}) collective-permute-start(f32[2,128,256]{2,1,0:T(8,128)S(1)} %get-tuple-element.13), channel_id=1, source_target_pairs={{0,1},{1,0},{2,3},{3,2},{4,5},{5,4},{6,7},{7,6},{8,9},{9,8},{10,11... | collective-permute-start | bytes 786440 | tf_op jit(solution)/shard_map/ppermute | solution.py:63
  33.3 8.9 %collective-permute-start.6 = (f32[2,128,256]{2,1,0:T(8,128)S(1)}, f32[2,128,256]{2,1,0:T(8,128)S(1)}, u32[]{:S(2)}, u32[]{:S(2)}) collective-permute-start(f32[2,128,256]{2,1,0:T(8,128)S(1)} %get-tuple-element.13), channel_id=1, source_target_pairs={{1,2},{2,1},{3,0},{0,3},{5,6},{6,5},{7,4},{4,7},{9,10},{10,9},{11,... | collective-permute-start | bytes 786440 | tf_op jit(solution)/shard_map/ppermute | solution.py:62
  33.9 8.5 %collective-permute-start.10 = (f32[2,128,256]{2,1,0:T(8,128)S(1)}, f32[2,128,256]{2,1,0:T(8,128)S(1)}, u32[]{:S(2)}, u32[]{:S(2)}) collective-permute-start(f32[2,128,256]{2,1,0:T(8,128)S(1)} %get-tuple-element.23), channel_id=1, source_target_pairs={{0,1},{1,0},{2,3},{3,2},{4,5},{5,4},{6,7},{7,6},{8,9},{9,8},{10,11... | collective-permute-start | bytes 786440 | tf_op jit(solution)/shard_map/ppermute | solution.py:63
  33.9 13.4 %collective-permute-start.9 = (f32[2,128,256]{2,1,0:T(8,128)S(1)}, f32[2,128,256]{2,1,0:T(8,128)S(1)}, u32[]{:S(2)}, u32[]{:S(2)}) collective-permute-start(f32[2,128,256]{2,1,0:T(8,128)S(1)} %get-tuple-element.23), channel_id=1, source_target_pairs={{1,2},{2,1},{3,0},{0,3},{5,6},{6,5},{7,4},{4,7},{9,10},{10,9},{11,... | collective-permute-start | bytes 786440 | tf_op jit(solution)/shard_map/ppermute | solution.py:62
  47.8 10.3 %collective-permute-start.8 = (f32[2,128,256]{2,1,0:T(8,128)S(1)}, f32[2,128,256]{2,1,0:T(8,128)S(1)}, u32[]{:S(2)}, u32[]{:S(2)}) collective-permute-start(f32[2,128,256]{2,1,0:T(8,128)S(1)} %get-tuple-element.21), channel_id=1, source_target_pairs={{0,4},{4,8},{8,12},{12,16},{16,20},{20,24},{24,28},{1,5},{5,9},{9,... | collective-permute-start | bytes 786440 | tf_op jit(solution)/shard_map/ppermute | solution.py:42
  50.0 13.7 %collective-permute-start.11 = (f32[2,128,256]{2,1,0:T(8,128)S(1)}, f32[2,128,256]{2,1,0:T(8,128)S(1)}, u32[]{:S(2)}, u32[]{:S(2)}) collective-permute-start(f32[2,128,256]{2,1,0:T(8,128)S(1)} %get-tuple-element.22), channel_id=1, source_target_pairs={{0,4},{4,8},{8,12},{12,16},{16,20},{20,24},{24,28},{1,5},{5,9},{9,... | collective-permute-start | bytes 786440 | tf_op jit(solution)/shard_map/ppermute | solution.py:42
  63.9 6.0 %collective-permute-start.13 = (f32[2,128,256]{2,1,0:T(8,128)S(1)}, f32[2,128,256]{2,1,0:T(8,128)S(1)}, u32[]{:S(2)}, u32[]{:S(2)}) collective-permute-start(f32[2,128,256]{2,1,0:T(8,128)S(1)} %get-tuple-element.9), channel_id=1, source_target_pairs={{0,1},{1,0},{2,3},{3,2},{4,5},{5,4},{6,7},{7,6},{8,9},{9,8},{10,11... | collective-permute-start | bytes 786440 | tf_op jit(solution)/shard_map/ppermute | solution.py:63
  65.2 8.9 %collective-permute-start.12 = (f32[2,128,256]{2,1,0:T(8,128)S(1)}, f32[2,128,256]{2,1,0:T(8,128)S(1)}, u32[]{:S(2)}, u32[]{:S(2)}) collective-permute-start(f32[2,128,256]{2,1,0:T(8,128)S(1)} %get-tuple-element.9), channel_id=1, source_target_pairs={{1,2},{2,1},{3,0},{0,3},{5,6},{6,5},{7,4},{4,7},{9,10},{10,9},{11,... | collective-permute-start | bytes 786440 | tf_op jit(solution)/shard_map/ppermute | solution.py:62
  65.4 8.8 %collective-permute-start.15 = (f32[2,128,256]{2,1,0:T(8,128)S(1)}, f32[2,128,256]{2,1,0:T(8,128)S(1)}, u32[]{:S(2)}, u32[]{:S(2)}) collective-permute-start(f32[2,128,256]{2,1,0:T(8,128)S(1)} %get-tuple-element.56), channel_id=1, source_target_pairs={{0,1},{1,0},{2,3},{3,2},{4,5},{5,4},{6,7},{7,6},{8,9},{9,8},{10,11... | collective-permute-start | bytes 786440 | tf_op jit(solution)/shard_map/ppermute | solution.py:63
  65.8 13.0 %collective-permute-start.14 = (f32[2,128,256]{2,1,0:T(8,128)S(1)}, f32[2,128,256]{2,1,0:T(8,128)S(1)}, u32[]{:S(2)}, u32[]{:S(2)}) collective-permute-start(f32[2,128,256]{2,1,0:T(8,128)S(1)} %get-tuple-element.56), channel_id=1, source_target_pairs={{1,2},{2,1},{3,0},{0,3},{5,6},{6,5},{7,4},{4,7},{9,10},{10,9},{11,... | collective-permute-start | bytes 786440 | tf_op jit(solution)/shard_map/ppermute | solution.py:62
  79.4 5.2 %collective-permute-start.17 = (f32[2,128,256]{2,1,0:T(8,128)S(1)}, f32[2,128,256]{2,1,0:T(8,128)S(1)}, u32[]{:S(2)}, u32[]{:S(2)}) collective-permute-start(f32[2,128,256]{2,1,0:T(8,128)S(1)} %get-tuple-element.5), channel_id=1, source_target_pairs={{0,1},{1,0},{2,3},{3,2},{4,5},{5,4},{6,7},{7,6},{8,9},{9,8},{10,11... | collective-permute-start | bytes 786440 | tf_op jit(solution)/shard_map/ppermute | solution.py:63
  79.5 8.9 %collective-permute-start.16 = (f32[2,128,256]{2,1,0:T(8,128)S(1)}, f32[2,128,256]{2,1,0:T(8,128)S(1)}, u32[]{:S(2)}, u32[]{:S(2)}) collective-permute-start(f32[2,128,256]{2,1,0:T(8,128)S(1)} %get-tuple-element.5), channel_id=1, source_target_pairs={{1,2},{2,1},{3,0},{0,3},{5,6},{6,5},{7,4},{4,7},{9,10},{10,9},{11,... | collective-permute-start | bytes 786440 | tf_op jit(solution)/shard_map/ppermute | solution.py:62
  80.0 8.4 %collective-permute-start.19 = (f32[2,128,256]{2,1,0:T(8,128)S(1)}, f32[2,128,256]{2,1,0:T(8,128)S(1)}, u32[]{:S(2)}, u32[]{:S(2)}) collective-permute-start(f32[2,128,256]{2,1,0:T(8,128)S(1)} %get-tuple-element.52), channel_id=1, source_target_pairs={{0,1},{1,0},{2,3},{3,2},{4,5},{5,4},{6,7},{7,6},{8,9},{9,8},{10,11... | collective-permute-start | bytes 786440 | tf_op jit(solution)/shard_map/ppermute | solution.py:63
  80.1 13.4 %collective-permute-start.18 = (f32[2,128,256]{2,1,0:T(8,128)S(1)}, f32[2,128,256]{2,1,0:T(8,128)S(1)}, u32[]{:S(2)}, u32[]{:S(2)}) collective-permute-start(f32[2,128,256]{2,1,0:T(8,128)S(1)} %get-tuple-element.52), channel_id=1, source_target_pairs={{1,2},{2,1},{3,0},{0,3},{5,6},{6,5},{7,4},{4,7},{9,10},{10,9},{11,... | collective-permute-start | bytes 786440 | tf_op jit(solution)/shard_map/ppermute | solution.py:62
